TPU v7x, 32 devices: a whole 2x2x4 slice. The times are simulated.
32 devices in a mesh: row: 8 (over z, y), col: 4 (over x, core).
Axes of the slice: x: 2, y: 2, z: 4, core: 2. Of those that a mesh axis runs over, the one named last changes fastest.
Arguments:
- inv_blocks: bfloat16 [2048, 2048], P('row', 'col'), may hold values from -0.125 to 0.125
- factor: bfloat16 [4, 2048, 128], P('col', 'row'), may hold values from -2.3125 to 2.3125
- pattern: int32 [4, 16], P('col', 'row'), may hold values from 0 to 1, as said below
- diag_inv: float32 [4, 128, 128], P(None, 'row', 'col'), may hold values from -12 to 12
Outputs:
- inverse_panel: bfloat16 [4, 128, 2048], P(None, 'col', 'row')
- diag_block: float32 [4, 128, 128], P(None, 'row', 'col')
Inputs may be any that keep to these rules, and one draw needn't show every extreme that they name: pattern is 0 or 1; each supernode has its own share of 1s.
All inputs are finite; a program needn't handle non-finite values.
Results may differ from a plain program's by a relative error of at most 0.0005.
Values may be sent and summed in bfloat16 or wider, within the bound.
No kernel may reach another device: no remote copies, remote signals or barrier semaphores. Data moves between devices by JAX's collectives and lax.ppermute only.
A program may use at most 64 MiB of HBM per device.

v0:
```python
import functools

import jax
import jax.numpy as jnp
from jax import lax
from jax.experimental import pallas as pl
from jax.experimental.pallas import tpu as pltpu
from jax.sharding import PartitionSpec as P


VMEM = pl.BlockSpec(memory_space=pltpu.VMEM)
PARAMS = pltpu.CompilerParams(vmem_limit_bytes=16 * 2**20)
LANES = 128


def in_hbm(array):
    return pltpu.with_memory_space_constraint(array, pltpu.HBM)


def swap(block, axis, distance):
    size = lax.axis_size(axis)
    return lax.ppermute(block, axis, [(i, i ^ distance) for i in range(size)])


def mask_kernel(pattern_ref, factor_ref, own_ref, keep_ref, rows_ref, sem):
    width = factor_ref.shape[2]
    copies = (
        pltpu.make_async_copy(factor_ref, rows_ref, sem.at[0]),
        pltpu.make_async_copy(pattern_ref, keep_ref, sem.at[1]),
    )
    for copy in copies:
        copy.start()
    for copy in copies:
        copy.wait()
    for block in range(keep_ref.shape[1]):
        rows = pl.ds(block * width, width)
        keep = keep_ref[0, block].astype(jnp.float32).astype(jnp.bfloat16)
        own_ref[rows, :] = rows_ref[0, rows, :] * keep


def add_products(total, blocks, level_ref, half):
    n_col = len(blocks)
    col = lax.axis_index("col")
    rows = level_ref.shape[1]
    pairs = blocks[0].shape[1] // (2 * rows)
    for distance in range(n_col):
        for pair in range(pairs):
            start = pl.multiple_of((2 * pair + half) * rows, rows)
            part = jnp.dot(
                blocks[distance][:, pl.ds(start, rows)],
                level_ref[(col ^ distance) * pairs + pair],
                preferred_element_type=jnp.float32,
            )
            total = part if total is None else total + part
    return total


def near_kernel(n_col, *refs):
    blocks, (level_ref, total_ref) = refs[:n_col], refs[n_col:]
    total_ref[...] = add_products(None, blocks, level_ref, lax.axis_index("row") % 2)


def far_kernel(n_col, dense, *refs):
    blocks = refs[:n_col]
    level_ref, near_ref, own_ref = refs[n_col : n_col + 3]
    packed_ref = refs[n_col + 3]
    sends = refs[n_col + 4 : 2 * n_col + 4]
    turned_ref, inner_ref = refs[2 * n_col + 4 :]
    col = lax.axis_index("col")
    total = add_products(near_ref[...], blocks, level_ref, 1 - lax.axis_index("row") % 2)

    tall = turned_ref.shape[0] // n_col
    turned_ref[...] = jnp.transpose(-total).astype(jnp.bfloat16)
    for distance in range(n_col):
        start = pl.multiple_of((col ^ distance) * tall, tall)
        sends[distance][...] = turned_ref[pl.ds(start, tall), :]

    high = total.astype(jnp.bfloat16)
    low = (total - high.astype(jnp.float32)).astype(jnp.bfloat16)
    own = own_ref[...]
    dims = (((0,), (0,)), ((), ()))
    inner = lax.dot_general(own, high, dims, preferred_element_type=jnp.float32)
    inner += lax.dot_general(own, low, dims, preferred_element_type=jnp.float32)
    if not dense:
        packed_ref[...] = inner
        return
    inner_ref[...] = inner
    lane = lax.broadcasted_iota(jnp.int32, (8, LANES), 1) // 32
    for a in range(4):
        parts = [inner_ref[pl.ds(4 * a + b, 8, stride=16), :] for b in range(4)]
        for owner in range(4):
            piece = parts[owner]
            for b in range(4):
                if b != owner:
                    turned = pltpu.roll(parts[b], (b - owner) % 4 * 32, 1)
                    piece = jnp.where(lane == b, turned, piece)
            packed_ref[pl.ds(4 * owner + a, 8, stride=16), :] = piece


def close_kernel(packed_ref, diag_ref, out_ref):
    total = packed_ref[pl.ds(0, 16), :]
    for row in range(1, 8):
        total += packed_ref[pl.ds(16 * row, 16), :]
    for b in range(4):
        part = pltpu.roll(total, (4 - b) % 4 * 32, 1) if b else total
        rows = pl.ds(b, 16, stride=4)
        out_ref[rows, :] = diag_ref[rows, :] + part[:, :32]


def on_device(inv_blocks, factor, pattern, diag_inv):
    n_row = lax.axis_size("row")
    n_col = lax.axis_size("col")
    rows, width = factor.shape[1:]
    tall, wide = width // n_row, width // n_col
    dense = (width, n_row, n_col) == (LANES, 8, 4)
    high = lax.axis_index("row") // 2
    shape = jax.ShapeDtypeStruct

    own = pl.pallas_call(
        mask_kernel,
        out_shape=shape((rows, width), jnp.bfloat16),
        in_specs=[pl.BlockSpec(memory_space=pltpu.HBM)] * 2,
        out_specs=VMEM,
        scratch_shapes=[
            pltpu.SMEM(pattern.shape, pattern.dtype),
            pltpu.VMEM(factor.shape, factor.dtype),
            pltpu.SemaphoreType.DMA((2,)),
        ],
        compiler_params=PARAMS,
        name="mask",
    )(in_hbm(pattern), in_hbm(factor))

    blocks = [None] * n_col
    blocks[0] = inv_blocks
    for distance in range(2, n_col, 2):
        blocks[distance] = swap(inv_blocks, "col", distance)
    for distance in range(0, n_col, 2):
        blocks[distance + 1] = swap(blocks[distance], "col", 1)

    near = jnp.zeros((n_row // 2, rows, width), jnp.bfloat16)
    far = jnp.zeros((n_row // 2, rows, width), jnp.bfloat16)
    for distance in range(0, n_row, 2):
        held = swap(own, "row", distance) if distance else own
        place = high ^ (distance // 2)
        near = lax.dynamic_update_index_in_dim(near, held, place, 0)
        held = swap(held, "row", 1)
        far = lax.dynamic_update_index_in_dim(far, held, place, 0)

    total = pl.pallas_call(
        functools.partial(near_kernel, n_col),
        out_shape=shape((rows, width), jnp.float32),
        in_specs=[VMEM] * (n_col + 1),
        out_specs=VMEM,
        compiler_params=PARAMS,
        name="near",
    )(*blocks, near)
    packed, *sends = pl.pallas_call(
        functools.partial(far_kernel, n_col, dense),
        out_shape=[shape((width, width), jnp.float32)]
        + [shape((wide, rows), jnp.bfloat16)] * n_col,
        in_specs=[VMEM] * (n_col + 3),
        out_specs=[VMEM] * (n_col + 1),
        scratch_shapes=[
            pltpu.VMEM((width, rows), jnp.bfloat16),
            pltpu.VMEM((width, width), jnp.float32),
        ],
        compiler_params=PARAMS,
        name="far",
    )(*blocks, far, total, own)

    col = lax.axis_index("col")
    panel = jnp.zeros((n_col, wide, rows), jnp.bfloat16)
    for distance in range(n_col):
        piece = sends[distance]
        if distance:
            piece = swap(piece, "col", distance)
        panel = lax.dynamic_update_index_in_dim(panel, piece, col ^ distance, 0)

    axes = ("row", "col")
    if dense:
        packed = packed.reshape(n_row * n_col, 4, LANES)
        packed = lax.all_to_all(packed, axes, 0, 0, tiled=True)
        diag_block = pl.pallas_call(
            close_kernel,
            out_shape=shape((n_col * tall, wide), jnp.float32),
            in_specs=[VMEM, VMEM],
            out_specs=VMEM,
            compiler_params=PARAMS,
            name="close",
        )(packed.reshape(width, width), diag_inv.reshape(n_col * tall, wide))
        return panel, diag_block.reshape(n_col, tall, wide)
    packed = packed.reshape(n_row, tall, n_col, wide).transpose(0, 2, 1, 3)
    packed = packed.reshape(n_row * n_col, 1, tall * wide)
    packed = lax.all_to_all(packed, axes, 0, 0, tiled=True)
    return panel, diag_inv + packed.reshape(n_row, n_col, tall, wide).sum(0)


def solution(mesh):
    return jax.shard_map(
        on_device,
        mesh=mesh,
        in_specs=(P("row", "col"), P("col", "row", None), P("col", "row"), P(None, "row", "col")),
        out_specs=(P(None, "col", "row"), P(None, "row", "col")),
        check_vma=False,
    )
```

profile of v0, /device:TPU:0, one launch (start us, length us, event | category | flops | bytes accessed | tf_op | source)
XLA Modules:
  0.0 35.0 jit_solution(11810444774836301953)
XLA Ops:
  0.6 0.9 %mask.1 = bf16[256,128]{1,0:T(8,128)(2,1)S(1)} custom-call(s32[1,2]{1,0:T(1,128)} %pattern_ref.1, bf16[1,256,128]{2,1,0:T(8,128)(2,1)} %factor_ref.1), custom_call_target="tpu_custom_call" | custom-call | tf_op jit(solution)/shard_map/mask/pallas_call | solution.py:119
  1.5 0.0 copy-start
  1.5 5.1 %collective-permute-start.8 = (bf16[256,128]{1,0:T(8,128)(2,1)S(1)}, bf16[256,128]{1,0:T(8,128)(2,1)S(1)}, u32[]{:S(2)}, u32[]{:S(2)}) collective-permute-start(bf16[256,128]{1,0:T(8,128)(2,1)S(1)} %mask.1), channel_id=1, source_target_pairs={{0,24},{4,28},{8,16},{12,20},{16,8},{20,12},{24,0},{28,4},{1,25},{... | collective-permute-start | bytes 196616 | tf_op jit(solution)/shard_map/ppermute | solution.py:22
  6.7 0.0 collective-permute-start.6
  6.7 0.6 %collective-permute-start.4 = (bf16[256,128]{1,0:T(8,128)(2,1)S(1)}, bf16[256,128]{1,0:T(8,128)(2,1)S(1)}, u32[]{:S(2)}, u32[]{:S(2)}) collective-permute-start(bf16[256,128]{1,0:T(8,128)(2,1)S(1)} %mask.1), channel_id=1, source_target_pairs={{0,8},{4,12},{8,0},{12,4},{16,24},{20,28},{24,16},{28,20},{1,9},{5... | collective-permute-start | bytes 196616 | tf_op jit(solution)/shard_map/ppermute | solution.py:22
  7.3 1.7 %collective-permute-start.3 = (bf16[256,128]{1,0:T(8,128)(2,1)S(1)}, bf16[256,128]{1,0:T(8,128)(2,1)S(1)}, u32[]{:S(2)}, u32[]{:S(2)}) collective-permute-start(bf16[256,128]{1,0:T(8,128)(2,1)S(1)} %mask.1), channel_id=1, source_target_pairs={{0,4},{4,0},{8,12},{12,8},{16,20},{20,16},{24,28},{28,24},{1,5},{5... | collective-permute-start | bytes 196616 | tf_op jit(solution)/shard_map/ppermute | solution.py:22
  9.0 1.5 %collective-permute-start.1 = (bf16[256,512]{1,0:T(8,128)(2,1)}, bf16[256,512]{1,0:T(8,128)(2,1)S(1)}, u32[]{:S(2)}, u32[]{:S(2)}) collective-permute-start(bf16[256,512]{1,0:T(8,128)(2,1)} %refs_0_.2), channel_id=1, source_target_pairs={{0,2},{1,3},{2,0},{3,1},{4,6},{5,7},{6,4},{7,5},{8,10},{9,11},{10,... | collective-permute-start | bytes 786440 | tf_op jit(solution)/shard_map/ppermute | solution.py:22
  10.6 0.0 collective-permute-done.8
  10.6 0.1 collective-permute-start
  10.7 1.6 %collective-permute-done.6 = bf16[256,128]{1,0:T(8,128)(2,1)S(1)} collective-permute-done((bf16[256,128]{1,0:T(8,128)(2,1)S(1)}, bf16[256,128]{1,0:T(8,128)(2,1)S(1)}, u32[]{:S(2)}, u32[]{:S(2)}) %collective-permute-start.6) | collective-permute-done | bytes 65568 | tf_op jit(solution)/shard_map/ppermute | solution.py:22
  12.3 1.5 %collective-permute-start.9 = (bf16[256,128]{1,0:T(8,128)(2,1)S(1)}, bf16[256,128]{1,0:T(8,128)(2,1)S(1)}, u32[]{:S(2)}, u32[]{:S(2)}) collective-permute-start(bf16[256,128]{1,0:T(8,128)(2,1)S(1)} %collective-permute-done.8), channel_id=1, source_target_pairs={{0,4},{4,0},{8,12},{12,8},{16,20},{20,16},{24,28},{28,24},{1,5},{5... | collective-permute-start | bytes 196616 | tf_op jit(solution)/shard_map/ppermute | solution.py:22
  13.8 0.0 collective-permute-done.4
  13.8 0.5 %collective-permute-start.7 = (bf16[256,128]{1,0:T(8,128)(2,1)S(1)}, bf16[256,128]{1,0:T(8,128)(2,1)S(1)}, u32[]{:S(2)}, u32[]{:S(2)}) collective-permute-start(bf16[256,128]{1,0:T(8,128)(2,1)S(1)} %collective-permute-done.6), channel_id=1, source_target_pairs={{0,4},{4,0},{8,12},{12,8},{16,20},{20,16},{24,28},{28,24},{1,5},{5... | collective-permute-start | bytes 196616 | tf_op jit(solution)/shard_map/ppermute | solution.py:22
  14.3 0.0 collective-permute-done.3
  14.3 1.5 %collective-permute-start.5 = (bf16[256,128]{1,0:T(8,128)(2,1)S(1)}, bf16[256,128]{1,0:T(8,128)(2,1)S(1)}, u32[]{:S(2)}, u32[]{:S(2)}) collective-permute-start(bf16[256,128]{1,0:T(8,128)(2,1)S(1)} %collective-permute-done.4), channel_id=1, source_target_pairs={{0,4},{4,0},{8,12},{12,8},{16,20},{20,16},{24,28},{28,24},{1,5},{5... | collective-permute-start | bytes 196616 | tf_op jit(solution)/shard_map/ppermute | solution.py:22
  16.0 3.4 %collective-permute-done.5 = bf16[256,128]{1,0:T(8,128)(2,1)S(1)} collective-permute-done((bf16[256,128]{1,0:T(8,128)(2,1)S(1)}, bf16[256,128]{1,0:T(8,128)(2,1)S(1)}, u32[]{:S(2)}, u32[]{:S(2)}) %collective-permute-start.5) | collective-permute-done | bytes 65568 | tf_op jit(solution)/shard_map/ppermute | solution.py:22
  19.4 0.0 collective-permute-done.1.refs_2_
  19.4 0.1 collective-permute-start.2
  19.5 0.0 collective-permute-done.7
  19.5 0.0 collective-permute-done.9
  19.5 0.0 collective-permute-done.refs_1_
  19.5 1.4 %collective-permute-done.2.refs_3_ = bf16[256,512]{1,0:T(8,128)(2,1)S(1)} collective-permute-done((bf16[256,512]{1,0:T(8,128)(2,1)S(1)}, bf16[256,512]{1,0:T(8,128)(2,1)S(1)}, u32[]{:S(2)}, u32[]{:S(2)}) %collective-permute-start.2) | collective-permute-done | bytes 262176 | tf_op jit(solution)/shard_map/ppermute | solution.py:22
  21.0 0.3 near.1
  21.3 1.3 %far.1 = (bf16[4,32,256]{2,1,0:T(8,128)(2,1)S(1)}, bf16[32,256]{1,0:T(8,128)(2,1)S(1)}, bf16[32,256]{1,0:T(8,128)(2,1)S(1)}, bf16[32,256]{1,0:T(8,128)(2,1)S(1)}, f32[128,128]{1,0:T(8,128)}) fusion(bf16[4,32,256]{2,1,0:T(8,128)(2,1)S(1)} %broadcast_in_dim.41, s32[]{:T(128)S(6)} %select_n.40, bf16[256,512]{1,0:T(8,128)(2,1)S(1)} %copy-done, ...), kind=kCustom, calls=%fused_computation.11 | custom fusion | bytes 1638404 | tf_op jit(solution)/shard_map/far/pallas_call | solution.py:157
  22.5 0.1 collective-permute-start.10
  22.7 4.2 %all-to-all-start = ((f32[32,4,128]{2,1,0:T(4,128)}), f32[32,4,128]{2,1,0:T(4,128)S(1)}, u32[]{:S(2)}, u32[]{:S(2)}) async-start(f32[32,4,128]{2,1,0:T(4,128)} %bitcast.12), calls=%async_computation | async-start | bytes 131072 | tf_op jit(solution)/shard_map/all_to_all | solution.py:182
  26.9 1.8 %collective-permute-start.11 = (bf16[32,256]{1,0:T(8,128)(2,1)S(1)}, bf16[32,256]{1,0:T(8,128)(2,1)S(1)}, u32[]{:S(2)}, u32[]{:S(2)}) collective-permute-start(bf16[32,256]{1,0:T(8,128)(2,1)S(1)} %get-tuple-element.17), channel_id=1, source_target_pairs={{0,2},{1,3},{2,0},{3,1},{4,6},{5,7},{6,4},{7,5},{8,10},{9,11},{10,... | collective-permute-start | bytes 49160 | tf_op jit(solution)/shard_map/ppermute | solution.py:22
  28.7 0.0 copy-start.1
  28.7 2.0 %collective-permute-done.11 = bf16[32,256]{1,0:T(8,128)(2,1)S(1)} collective-permute-done((bf16[32,256]{1,0:T(8,128)(2,1)S(1)}, bf16[32,256]{1,0:T(8,128)(2,1)S(1)}, u32[]{:S(2)}, u32[]{:S(2)}) %collective-permute-start.11) | collective-permute-done | bytes 16416 | tf_op jit(solution)/shard_map/ppermute | solution.py:22
  30.7 1.4 %collective-permute-done.12 = bf16[32,256]{1,0:T(8,128)(2,1)S(1)} collective-permute-done((bf16[32,256]{1,0:T(8,128)(2,1)S(1)}, bf16[32,256]{1,0:T(8,128)(2,1)S(1)}, u32[]{:S(2)}, u32[]{:S(2)}) %collective-permute-start.12) | collective-permute-done | bytes 16416 | tf_op jit(solution)/shard_map/ppermute | solution.py:22
  32.1 2.2 %all-to-all-done = f32[32,4,128]{2,1,0:T(4,128)S(1)} async-done(((f32[32,4,128]{2,1,0:T(4,128)}), f32[32,4,128]{2,1,0:T(4,128)S(1)}, u32[]{:S(2)}, u32[]{:S(2)}) %all-to-all-start) | async-done | bytes 65568 | tf_op jit(solution)/shard_map/all_to_all | solution.py:182
  34.3 0.7 %close.1 = f32[64,32]{1,0:T(8,128)} custom-call(f32[128,128]{1,0:T(8,128)S(1)} %bitcast.28, f32[64,32]{1,0:T(8,128)S(1)} %bitcast.29), custom_call_target="tpu_custom_call" | custom-call | tf_op jit(solution)/shard_map/close/pallas_call | solution.py:183
  (20 shorter events, 0.2 us)
Async XLA Ops:
  1.5 9.1 %copy-start = (bf16[256,512]{1,0:T(8,128)(2,1)S(1)}, bf16[256,512]{1,0:T(8,128)(2,1)}, u32[]{:S(2)}) copy-start(bf16[256,512]{1,0:T(8,128)(2,1)} %refs_0_.2) | copy-start | bytes 786436
  1.5 9.0 %collective-permute-start.8 = (bf16[256,128]{1,0:T(8,128)(2,1)S(1)}, bf16[256,128]{1,0:T(8,128)(2,1)S(1)}, u32[]{:S(2)}, u32[]{:S(2)}) collective-permute-start(bf16[256,128]{1,0:T(8,128)(2,1)S(1)} %mask.1), channel_id=1, source_target_pairs={{0,24},{4,28},{8,16},{12,20},{16,8},{20,12},{24,0},{28,4},{1,25},{... | collective-permute-start | bytes 196616 | tf_op jit(solution)/shard_map/ppermute | solution.py:22
  6.7 5.6 %collective-permute-start.6 = (bf16[256,128]{1,0:T(8,128)(2,1)S(1)}, bf16[256,128]{1,0:T(8,128)(2,1)S(1)}, u32[]{:S(2)}, u32[]{:S(2)}) collective-permute-start(bf16[256,128]{1,0:T(8,128)(2,1)S(1)} %mask.1), channel_id=1, source_target_pairs={{0,16},{4,20},{8,24},{12,28},{16,0},{20,4},{24,8},{28,12},{1,17},{... | collective-permute-start | bytes 196616 | tf_op jit(solution)/shard_map/ppermute | solution.py:22
  6.7 7.1 %collective-permute-start.4 = (bf16[256,128]{1,0:T(8,128)(2,1)S(1)}, bf16[256,128]{1,0:T(8,128)(2,1)S(1)}, u32[]{:S(2)}, u32[]{:S(2)}) collective-permute-start(bf16[256,128]{1,0:T(8,128)(2,1)S(1)} %mask.1), channel_id=1, source_target_pairs={{0,8},{4,12},{8,0},{12,4},{16,24},{20,28},{24,16},{28,20},{1,9},{5... | collective-permute-start | bytes 196616 | tf_op jit(solution)/shard_map/ppermute | solution.py:22
  7.3 7.0 %collective-permute-start.3 = (bf16[256,128]{1,0:T(8,128)(2,1)S(1)}, bf16[256,128]{1,0:T(8,128)(2,1)S(1)}, u32[]{:S(2)}, u32[]{:S(2)}) collective-permute-start(bf16[256,128]{1,0:T(8,128)(2,1)S(1)} %mask.1), channel_id=1, source_target_pairs={{0,4},{4,0},{8,12},{12,8},{16,20},{20,16},{24,28},{28,24},{1,5},{5... | collective-permute-start | bytes 196616 | tf_op jit(solution)/shard_map/ppermute | solution.py:22
  9.0 10.4 %collective-permute-start.1 = (bf16[256,512]{1,0:T(8,128)(2,1)}, bf16[256,512]{1,0:T(8,128)(2,1)S(1)}, u32[]{:S(2)}, u32[]{:S(2)}) collective-permute-start(bf16[256,512]{1,0:T(8,128)(2,1)} %refs_0_.2), channel_id=1, source_target_pairs={{0,2},{1,3},{2,0},{3,1},{4,6},{5,7},{6,4},{7,5},{8,10},{9,11},{10,... | collective-permute-start | bytes 786440 | tf_op jit(solution)/shard_map/ppermute | solution.py:22
  10.6 8.9 %collective-permute-start = (bf16[256,512]{1,0:T(8,128)(2,1)S(1)}, bf16[256,512]{1,0:T(8,128)(2,1)S(1)}, u32[]{:S(2)}, u32[]{:S(2)}) collective-permute-start(bf16[256,512]{1,0:T(8,128)(2,1)S(1)} %copy-done), channel_id=1, source_target_pairs={{0,1},{1,0},{2,3},{3,2},{4,5},{5,4},{6,7},{7,6},{8,9},{9,8},{10,11... | collective-permute-start | bytes 786440 | tf_op jit(solution)/shard_map/ppermute | solution.py:22
  12.3 7.2 %collective-permute-start.9 = (bf16[256,128]{1,0:T(8,128)(2,1)S(1)}, bf16[256,128]{1,0:T(8,128)(2,1)S(1)}, u32[]{:S(2)}, u32[]{:S(2)}) collective-permute-start(bf16[256,128]{1,0:T(8,128)(2,1)S(1)} %collective-permute-done.8), channel_id=1, source_target_pairs={{0,4},{4,0},{8,12},{12,8},{16,20},{20,16},{24,28},{28,24},{1,5},{5... | collective-permute-start | bytes 196616 | tf_op jit(solution)/shard_map/ppermute | solution.py:22
  13.8 5.7 %collective-permute-start.7 = (bf16[256,128]{1,0:T(8,128)(2,1)S(1)}, bf16[256,128]{1,0:T(8,128)(2,1)S(1)}, u32[]{:S(2)}, u32[]{:S(2)}) collective-permute-start(bf16[256,128]{1,0:T(8,128)(2,1)S(1)} %collective-permute-done.6), channel_id=1, source_target_pairs={{0,4},{4,0},{8,12},{12,8},{16,20},{20,16},{24,28},{28,24},{1,5},{5... | collective-permute-start | bytes 196616 | tf_op jit(solution)/shard_map/ppermute | solution.py:22
  14.3 5.0 %collective-permute-start.5 = (bf16[256,128]{1,0:T(8,128)(2,1)S(1)}, bf16[256,128]{1,0:T(8,128)(2,1)S(1)}, u32[]{:S(2)}, u32[]{:S(2)}) collective-permute-start(bf16[256,128]{1,0:T(8,128)(2,1)S(1)} %collective-permute-done.4), channel_id=1, source_target_pairs={{0,4},{4,0},{8,12},{12,8},{16,20},{20,16},{24,28},{28,24},{1,5},{5... | collective-permute-start | bytes 196616 | tf_op jit(solution)/shard_map/ppermute | solution.py:22
  19.4 1.6 %collective-permute-start.2 = (bf16[256,512]{1,0:T(8,128)(2,1)S(1)}, bf16[256,512]{1,0:T(8,128)(2,1)S(1)}, u32[]{:S(2)}, u32[]{:S(2)}) collective-permute-start(bf16[256,512]{1,0:T(8,128)(2,1)S(1)} %collective-permute-done.1.refs_2_), channel_id=1, source_target_pairs={{0,1},{1,0},{2,3},{3,2},{4,5},{5,4},{6,7},{7,6},{8,9},{9,8},{10,11... | collective-permute-start | bytes 786440 | tf_op jit(solution)/shard_map/ppermute | solution.py:22
  22.5 6.2 %collective-permute-start.10 = (bf16[32,256]{1,0:T(8,128)(2,1)S(1)}, bf16[32,256]{1,0:T(8,128)(2,1)S(1)}, u32[]{:S(2)}, u32[]{:S(2)}) collective-permute-start(bf16[32,256]{1,0:T(8,128)(2,1)S(1)} %get-tuple-element.15), channel_id=1, source_target_pairs={{0,1},{1,0},{2,3},{3,2},{4,5},{5,4},{6,7},{7,6},{8,9},{9,8},{10,11... | collective-permute-start | bytes 49160 | tf_op jit(solution)/shard_map/ppermute | solution.py:22
  22.7 11.6 %all-to-all-start = ((f32[32,4,128]{2,1,0:T(4,128)}), f32[32,4,128]{2,1,0:T(4,128)S(1)}, u32[]{:S(2)}, u32[]{:S(2)}) async-start(f32[32,4,128]{2,1,0:T(4,128)} %bitcast.12), calls=%async_computation | async-start | bytes 131072 | tf_op jit(solution)/shard_map/all_to_all | solution.py:182
  26.9 3.8 %collective-permute-start.11 = (bf16[32,256]{1,0:T(8,128)(2,1)S(1)}, bf16[32,256]{1,0:T(8,128)(2,1)S(1)}, u32[]{:S(2)}, u32[]{:S(2)}) collective-permute-start(bf16[32,256]{1,0:T(8,128)(2,1)S(1)} %get-tuple-element.17), channel_id=1, source_target_pairs={{0,2},{1,3},{2,0},{3,1},{4,6},{5,7},{6,4},{7,5},{8,10},{9,11},{10,... | collective-permute-start | bytes 49160 | tf_op jit(solution)/shard_map/ppermute | solution.py:22
  28.7 3.4 %collective-permute-start.12 = (bf16[32,256]{1,0:T(8,128)(2,1)S(1)}, bf16[32,256]{1,0:T(8,128)(2,1)S(1)}, u32[]{:S(2)}, u32[]{:S(2)}) collective-permute-start(bf16[32,256]{1,0:T(8,128)(2,1)S(1)} %get-tuple-element.19), channel_id=1, source_target_pairs={{0,3},{1,2},{2,1},{3,0},{4,7},{5,6},{6,5},{7,4},{8,11},{9,10},{10,... | collective-permute-start | bytes 49160 | tf_op jit(solution)/shard_map/ppermute | solution.py:22
  28.7 5.6 %copy-start.1 = (f32[4,16,32]{2,1,0:T(8,128)S(1)}, f32[4,16,32]{2,1,0:T(8,128)}, u32[]{:S(2)}) copy-start(f32[4,16,32]{2,1,0:T(8,128)} %param.7) | copy-start | bytes 24580
  32.1 2.9 %copy-start.2 = (bf16[4,32,256]{2,1,0:T(8,128)(2,1)}, bf16[4,32,256]{2,1,0:T(8,128)(2,1)S(1)}, u32[]{:S(2)}) copy-start(bf16[4,32,256]{2,1,0:T(8,128)(2,1)S(1)} %bitcast_dynamic-update-slice_fusion.8) | copy-start | bytes 196612
where the time goes:
time: 35.2 us; the launch traced here: 35 us
  starting transfers between devices  18.8 us (53%)
  waiting for transfers between devices  12 us (34%)
  Pallas kernels  1.86 us (5%)
  local copies, waits for them, and re-layouts  1.5 us (4%)
  between operations  0.82 us (2%)
    ppermute x13, starting transfers between devices, swap(): return lax.ppermute(block, axis, [(i, i ^ distance) for i in range(size)])  14.6 us
    ppermute x13, waiting for transfers between devices, swap(): return lax.ppermute(block, axis, [(i, i ^ distance) for i in range(size)])  9.81 us
    all_to_all x1, starting transfers between devices, on_device(): packed = lax.all_to_all(packed, axes, 0, 0, tiled=True)  4.19 us
    all_to_all x1, waiting for transfers between devices, on_device(): packed = lax.all_to_all(packed, axes, 0, 0, tiled=True)  2.2 us
    pallas_call x1, local copies, waits for them, and re-layouts, on_device(): pl.pallas_call(functools.partial(far_kernel, n_col, dense), out_shape=[sh...  1.26 us
    pallas_call x1, Pallas kernels, on_device(): pl.pallas_call(mask_kernel, out_shape=shape((rows, width), jnp.bfloat16),...  0.88 us
  transfers between devices with their start and end apart: 14, of which 6 were waited for; matrix products, arithmetic and copies ran while one was open for 1% of the time, Pallas kernels for 0%

commit v1 on v0

--- a/solution.py
+++ b/solution.py
@@ -11,6 +11,7 @@
 VMEM = pl.BlockSpec(memory_space=pltpu.VMEM)
 PARAMS = pltpu.CompilerParams(vmem_limit_bytes=16 * 2**20)
 LANES = 128
+ROUTES = {1: (0, 1), 2: (0, 2), 3: (2, 1), 4: (0, 4), 5: (4, 1), 6: (4, 2), 7: (0, 7)}
 
 
 def in_hbm(array):
@@ -22,32 +23,40 @@
     return lax.ppermute(block, axis, [(i, i ^ distance) for i in range(size)])
 
 
-def mask_kernel(pattern_ref, factor_ref, own_ref, keep_ref, rows_ref, sem):
+def routes(distance, n_row):
+    if n_row == 8:
+        return ROUTES[distance]
+    return (distance - 1, 1) if distance % 2 else (0, distance)
+
+
+def mask_kernel(pattern_ref, factor_ref, inv_ref, own_ref, kept_ref, keep_ref, rows_ref, sem):
     width = factor_ref.shape[2]
+    kept = pltpu.make_async_copy(inv_ref, kept_ref, sem.at[2])
     copies = (
         pltpu.make_async_copy(factor_ref, rows_ref, sem.at[0]),
         pltpu.make_async_copy(pattern_ref, keep_ref, sem.at[1]),
     )
     for copy in copies:
         copy.start()
+    kept.start()
     for copy in copies:
         copy.wait()
     for block in range(keep_ref.shape[1]):
         rows = pl.ds(block * width, width)
         keep = keep_ref[0, block].astype(jnp.float32).astype(jnp.bfloat16)
         own_ref[rows, :] = rows_ref[0, rows, :] * keep
+    kept.wait()
 
 
 def add_products(total, blocks, level_ref, half):
-    n_col = len(blocks)
     col = lax.axis_index("col")
     rows = level_ref.shape[1]
     pairs = blocks[0].shape[1] // (2 * rows)
-    for distance in range(n_col):
+    for distance, block_ref in enumerate(blocks):
         for pair in range(pairs):
             start = pl.multiple_of((2 * pair + half) * rows, rows)
             part = jnp.dot(
-                blocks[distance][:, pl.ds(start, rows)],
+                block_ref[:, pl.ds(start, rows)],
                 level_ref[(col ^ distance) * pairs + pair],
                 preferred_element_type=jnp.float32,
             )
@@ -55,17 +64,26 @@
     return total
 
 
+def fill(level_ref, held_refs, first):
+    row = lax.axis_index("row")
+    for i, held_ref in enumerate(held_refs):
+        level_ref[(row ^ (2 * i + first)) // 2] = held_ref[...]
+
+
 def near_kernel(n_col, *refs):
-    blocks, (level_ref, total_ref) = refs[:n_col], refs[n_col:]
-    total_ref[...] = add_products(None, blocks, level_ref, lax.axis_index("row") % 2)
+    blocks, held, (total_ref, level_ref) = refs[:n_col], refs[n_col:-2], refs[-2:]
+    fill(level_ref, held, 0)
+    half = lax.axis_index("row") % 2
+    total_ref[...] = add_products(None, blocks, level_ref, half)
 
 
 def far_kernel(n_col, dense, *refs):
     blocks = refs[:n_col]
-    level_ref, near_ref, own_ref = refs[n_col : n_col + 3]
-    packed_ref = refs[n_col + 3]
-    sends = refs[n_col + 4 : 2 * n_col + 4]
-    turned_ref, inner_ref = refs[2 * n_col + 4 :]
+    near_ref, own_ref = refs[n_col : n_col + 2]
+    held, refs = refs[n_col + 2 : -4 - n_col], refs[-4 - n_col :]
+    packed_ref, sends = refs[0], refs[1 : 1 + n_col]
+    turned_ref, inner_ref, level_ref = refs[1 + n_col :]
+    fill(level_ref, held, 1)
     col = lax.axis_index("col")
     total = add_products(near_ref[...], blocks, level_ref, 1 - lax.axis_index("row") % 2)
 
@@ -113,60 +131,61 @@
     rows, width = factor.shape[1:]
     tall, wide = width // n_row, width // n_col
     dense = (width, n_row, n_col) == (LANES, 8, 4)
-    high = lax.axis_index("row") // 2
     shape = jax.ShapeDtypeStruct
 
-    own = pl.pallas_call(
+    own, kept = pl.pallas_call(
         mask_kernel,
-        out_shape=shape((rows, width), jnp.bfloat16),
-        in_specs=[pl.BlockSpec(memory_space=pltpu.HBM)] * 2,
-        out_specs=VMEM,
+        out_shape=[
+            shape((rows, width), jnp.bfloat16),
+            shape(inv_blocks.shape, jnp.bfloat16),
+        ],
+        in_specs=[pl.BlockSpec(memory_space=pltpu.HBM)] * 3,
+        out_specs=[VMEM] * 2,
         scratch_shapes=[
             pltpu.SMEM(pattern.shape, pattern.dtype),
             pltpu.VMEM(factor.shape, factor.dtype),
-            pltpu.SemaphoreType.DMA((2,)),
+            pltpu.SemaphoreType.DMA((3,)),
         ],
         compiler_params=PARAMS,
         name="mask",
-    )(in_hbm(pattern), in_hbm(factor))
+    )(in_hbm(pattern), in_hbm(factor), in_hbm(inv_blocks))
 
     blocks = [None] * n_col
-    blocks[0] = inv_blocks
+    blocks[0] = kept
     for distance in range(2, n_col, 2):
-        blocks[distance] = swap(inv_blocks, "col", distance)
+        blocks[distance] = swap(kept, "col", distance)
     for distance in range(0, n_col, 2):
         blocks[distance + 1] = swap(blocks[distance], "col", 1)
 
-    near = jnp.zeros((n_row // 2, rows, width), jnp.bfloat16)
-    far = jnp.zeros((n_row // 2, rows, width), jnp.bfloat16)
-    for distance in range(0, n_row, 2):
-        held = swap(own, "row", distance) if distance else own
-        place = high ^ (distance // 2)
-        near = lax.dynamic_update_index_in_dim(near, held, place, 0)
-        held = swap(held, "row", 1)
-        far = lax.dynamic_update_index_in_dim(far, held, place, 0)
-
+    held = {0: own}
+    for distance in sorted(range(1, n_row), key=lambda d: (routes(d, n_row)[0] != 0, d)):
+        relay, hop = routes(distance, n_row)
+        held[distance] = swap(held[relay], "row", hop)
+
+    level = pltpu.VMEM((n_row // 2, rows, width), jnp.bfloat16)
     total = pl.pallas_call(
         functools.partial(near_kernel, n_col),
         out_shape=shape((rows, width), jnp.float32),
-        in_specs=[VMEM] * (n_col + 1),
+        in_specs=[VMEM] * (n_col + n_row // 2),
         out_specs=VMEM,
+        scratch_shapes=[level],
         compiler_params=PARAMS,
         name="near",
-    )(*blocks, near)
+    )(*blocks, *(held[d] for d in range(0, n_row, 2)))
     packed, *sends = pl.pallas_call(
         functools.partial(far_kernel, n_col, dense),
         out_shape=[shape((width, width), jnp.float32)]
         + [shape((wide, rows), jnp.bfloat16)] * n_col,
-        in_specs=[VMEM] * (n_col + 3),
+        in_specs=[VMEM] * (n_col + 2 + n_row // 2),
         out_specs=[VMEM] * (n_col + 1),
         scratch_shapes=[
             pltpu.VMEM((width, rows), jnp.bfloat16),
             pltpu.VMEM((width, width), jnp.float32),
+            level,
         ],
         compiler_params=PARAMS,
         name="far",
-    )(*blocks, far, total, own)
+    )(*blocks, total, own, *(held[d] for d in range(1, n_row, 2)))
 
     col = lax.axis_index("col")
     panel = jnp.zeros((n_col, wide, rows), jnp.bfloat16)
@@ -196,10 +215,13 @@
 
 
 def solution(mesh):
-    return jax.shard_map(
+    step = jax.shard_map(
         on_device,
         mesh=mesh,
         in_specs=(P("row", "col"), P("col", "row", None), P("col", "row"), P(None, "row", "col")),
         out_specs=(P(None, "col", "row"), P(None, "row", "col")),
         check_vma=False,
     )
+    if dict(mesh.shape) != {"row": 8, "col": 4}:
+        return step
+    return step

time: 35.2 us -> 45.1 us (1.28)
  waiting for transfers between devices: 12 us -> 19.9 us
  starting transfers between devices: 18.8 us -> 20.9 us
    all_to_all x1, waiting for transfers between devices: 2.2 us -> 7.3 us  [on_device(): packed = lax.all_to_all(packed, axes, 0, 0, tiled=True)]
    ppermute x13, waiting for transfers between devices: 9.81 us -> 12.6 us  [swap(): return lax.ppermute(block, axis, [(i, i ^ distance) for i in range(size)])]
    ppermute x13, starting transfers between devices: 14.6 us -> 16.5 us  [swap(): return lax.ppermute(block, axis, [(i, i ^ distance) for i in range(size)])]
  transfers between devices with their start and end apart: 14 -> 14, of which waited for: 6 -> 6; matrix products, arithmetic and copies ran while one was open for 1% -> 0% of each run, Pallas kernels for 0% -> 1%
where the time goes in v1:
time: 45.1 us; the launch traced here: 44.9 us
  starting transfers between devices  20.9 us (46%)
  waiting for transfers between devices  19.9 us (44%)
  Pallas kernels  2.03 us (5%)
  local copies, waits for them, and re-layouts  1.32 us (3%)
  between operations  0.74 us (2%)
    ppermute x13, starting transfers between devices, swap(): return lax.ppermute(block, axis, [(i, i ^ distance) for i in range(size)])  16.5 us
    ppermute x13, waiting for transfers between devices, swap(): return lax.ppermute(block, axis, [(i, i ^ distance) for i in range(size)])  12.6 us
    all_to_all x1, waiting for transfers between devices, on_device(): packed = lax.all_to_all(packed, axes, 0, 0, tiled=True)  7.3 us
    all_to_all x1, starting transfers between devices, on_device(): packed = lax.all_to_all(packed, axes, 0, 0, tiled=True)  4.41 us
    pallas_call x1, local copies, waits for them, and re-layouts, on_device(): pl.pallas_call(functools.partial(far_kernel, n_col, dense), out_shape=[sh...  1.28 us
    pallas_call x1, Pallas kernels, on_device(): pl.pallas_call(mask_kernel, out_shape=[shape((rows, width), jnp.bfloat16)...  1.02 us
  transfers between devices with their start and end apart: 14, of which 6 were waited for; matrix products, arithmetic and copies ran while one was open for 0% of the time, Pallas kernels for 1%

profile of v1, /device:TPU:0, one launch (start us, length us, event | category | flops | bytes accessed | tf_op | source)
XLA Modules:
  0.0 44.9 jit_solution(5372377700807056127)
XLA Ops:
  0.6 1.0 %mask.1 = (bf16[256,128]{1,0:T(8,128)(2,1)S(1)}, bf16[256,512]{1,0:T(8,128)(2,1)S(1)}) custom-call(s32[1,2]{1,0:T(1,128)} %pattern_ref.1, bf16[1,256,128]{2,1,0:T(8,128)(2,1)} %factor_ref.1, bf16[256,512]{1,0:T(8,128)(2,1)} %inv_ref.1), custom_call_target="tpu_custom_call" | custom-call | tf_op jit(solution)/shard_map/mask/pallas_call | solution.py:136
  1.7 3.0 %collective-permute-start.1 = (bf16[256,512]{1,0:T(8,128)(2,1)S(1)}, bf16[256,512]{1,0:T(8,128)(2,1)S(1)}, u32[]{:S(2)}, u32[]{:S(2)}) collective-permute-start(bf16[256,512]{1,0:T(8,128)(2,1)S(1)} %get-tuple-element.9.refs_0_), channel_id=1, source_target_pairs={{0,2},{1,3},{2,0},{3,1},{4,6},{5,7},{6,4},{7,5},{8,10},{9,11},{10,... | collective-permute-start | bytes 786440 | tf_op jit(solution)/shard_map/ppermute | solution.py:23
  4.7 0.0 collective-permute-start
  4.7 6.3 %collective-permute-done.1.refs_2_ = bf16[256,512]{1,0:T(8,128)(2,1)S(1)} collective-permute-done((bf16[256,512]{1,0:T(8,128)(2,1)S(1)}, bf16[256,512]{1,0:T(8,128)(2,1)S(1)}, u32[]{:S(2)}, u32[]{:S(2)}) %collective-permute-start.1) | collective-permute-done | bytes 262176 | tf_op jit(solution)/shard_map/ppermute | solution.py:23
  11.0 0.0 collective-permute-start.2
  11.0 2.8 %collective-permute-start.4 = (bf16[256,128]{1,0:T(8,128)(2,1)S(1)}, bf16[256,128]{1,0:T(8,128)(2,1)S(1)}, u32[]{:S(2)}, u32[]{:S(2)}) collective-permute-start(bf16[256,128]{1,0:T(8,128)(2,1)S(1)} %get-tuple-element.10.refs_4_), channel_id=1, source_target_pairs={{0,16},{4,20},{8,24},{12,28},{16,0},{20,4},{24,8},{28,12},{1,17},{... | collective-permute-start | bytes 196616 | tf_op jit(solution)/shard_map/ppermute | solution.py:23
  13.8 1.6 %collective-permute-start.3 = (bf16[256,128]{1,0:T(8,128)(2,1)S(1)}, bf16[256,128]{1,0:T(8,128)(2,1)S(1)}, u32[]{:S(2)}, u32[]{:S(2)}) collective-permute-start(bf16[256,128]{1,0:T(8,128)(2,1)S(1)} %get-tuple-element.10.refs_4_), channel_id=1, source_target_pairs={{0,8},{4,12},{8,0},{12,4},{16,24},{20,28},{24,16},{28,20},{1,9},{5... | collective-permute-start | bytes 196616 | tf_op jit(solution)/shard_map/ppermute | solution.py:23
  15.4 2.4 %collective-permute-done.4.refs_6_ = bf16[256,128]{1,0:T(8,128)(2,1)S(1)} collective-permute-done((bf16[256,128]{1,0:T(8,128)(2,1)S(1)}, bf16[256,128]{1,0:T(8,128)(2,1)S(1)}, u32[]{:S(2)}, u32[]{:S(2)}) %collective-permute-start.4) | collective-permute-done | bytes 65568 | tf_op jit(solution)/shard_map/ppermute | solution.py:23
  17.9 0.9 %collective-permute-start.5 = (bf16[256,128]{1,0:T(8,128)(2,1)S(1)}, bf16[256,128]{1,0:T(8,128)(2,1)S(1)}, u32[]{:S(2)}, u32[]{:S(2)}) collective-permute-start(bf16[256,128]{1,0:T(8,128)(2,1)S(1)} %collective-permute-done.4.refs_6_), channel_id=1, source_target_pairs={{0,8},{4,12},{8,0},{12,4},{16,24},{20,28},{24,16},{28,20},{1,9},{5... | collective-permute-start | bytes 196616 | tf_op jit(solution)/shard_map/ppermute | solution.py:23
  18.8 1.5 %collective-permute-start.6 = (bf16[256,128]{1,0:T(8,128)(2,1)S(1)}, bf16[256,128]{1,0:T(8,128)(2,1)S(1)}, u32[]{:S(2)}, u32[]{:S(2)}) collective-permute-start(bf16[256,128]{1,0:T(8,128)(2,1)S(1)} %get-tuple-element.10.refs_4_), channel_id=1, source_target_pairs={{0,4},{4,0},{8,12},{12,8},{16,20},{20,16},{24,28},{28,24},{1,5},{5... | collective-permute-start | bytes 196616 | tf_op jit(solution)/shard_map/ppermute | solution.py:23
  20.3 0.0 collective-permute-done.3.refs_5_
  20.3 2.7 %collective-permute-start.9 = (bf16[256,128]{1,0:T(8,128)(2,1)S(1)}, bf16[256,128]{1,0:T(8,128)(2,1)S(1)}, u32[]{:S(2)}, u32[]{:S(2)}) collective-permute-start(bf16[256,128]{1,0:T(8,128)(2,1)S(1)} %get-tuple-element.10.refs_4_), channel_id=1, source_target_pairs={{0,28},{4,24},{8,20},{12,16},{16,12},{20,8},{24,4},{28,0},{1,29},{... | collective-permute-start | bytes 196616 | tf_op jit(solution)/shard_map/ppermute | solution.py:23
  23.0 0.0 collective-permute-done.5.refs_7_
  23.0 1.5 %collective-permute-start.8 = (bf16[256,128]{1,0:T(8,128)(2,1)S(1)}, bf16[256,128]{1,0:T(8,128)(2,1)S(1)}, u32[]{:S(2)}, u32[]{:S(2)}) collective-permute-start(bf16[256,128]{1,0:T(8,128)(2,1)S(1)} %collective-permute-done.4.refs_6_), channel_id=1, source_target_pairs={{0,4},{4,0},{8,12},{12,8},{16,20},{20,16},{24,28},{28,24},{1,5},{5... | collective-permute-start | bytes 196616 | tf_op jit(solution)/shard_map/ppermute | solution.py:23
  24.5 0.0 collective-permute-done.refs_1_
  24.5 0.5 %collective-permute-start.7 = (bf16[256,128]{1,0:T(8,128)(2,1)S(1)}, bf16[256,128]{1,0:T(8,128)(2,1)S(1)}, u32[]{:S(2)}, u32[]{:S(2)}) collective-permute-start(bf16[256,128]{1,0:T(8,128)(2,1)S(1)} %collective-permute-done.3.refs_5_), channel_id=1, source_target_pairs={{0,4},{4,0},{8,12},{12,8},{16,20},{20,16},{24,28},{28,24},{1,5},{5... | collective-permute-start | bytes 196616 | tf_op jit(solution)/shard_map/ppermute | solution.py:23
  25.0 0.0 collective-permute-done.2.refs_3_
  25.0 0.3 near.1
  25.4 0.0 collective-permute-done.6
  25.4 2.0 %collective-permute-done.9 = bf16[256,128]{1,0:T(8,128)(2,1)S(1)} collective-permute-done((bf16[256,128]{1,0:T(8,128)(2,1)S(1)}, bf16[256,128]{1,0:T(8,128)(2,1)S(1)}, u32[]{:S(2)}, u32[]{:S(2)}) %collective-permute-start.9) | collective-permute-done | bytes 65568 | tf_op jit(solution)/shard_map/ppermute | solution.py:23
  27.3 1.2 %collective-permute-done.8 = bf16[256,128]{1,0:T(8,128)(2,1)S(1)} collective-permute-done((bf16[256,128]{1,0:T(8,128)(2,1)S(1)}, bf16[256,128]{1,0:T(8,128)(2,1)S(1)}, u32[]{:S(2)}, u32[]{:S(2)}) %collective-permute-start.8) | collective-permute-done | bytes 65568 | tf_op jit(solution)/shard_map/ppermute | solution.py:23
  28.6 0.7 %collective-permute-done.7 = bf16[256,128]{1,0:T(8,128)(2,1)S(1)} collective-permute-done((bf16[256,128]{1,0:T(8,128)(2,1)S(1)}, bf16[256,128]{1,0:T(8,128)(2,1)S(1)}, u32[]{:S(2)}, u32[]{:S(2)}) %collective-permute-start.7) | collective-permute-done | bytes 65568 | tf_op jit(solution)/shard_map/ppermute | solution.py:23
  29.3 1.3 %far.1 = (bf16[4,32,256]{2,1,0:T(8,128)(2,1)S(1)}, bf16[32,256]{1,0:T(8,128)(2,1)S(1)}, bf16[32,256]{1,0:T(8,128)(2,1)S(1)}, bf16[32,256]{1,0:T(8,128)(2,1)S(1)}, f32[128,128]{1,0:T(8,128)}) fusion(bf16[4,32,256]{2,1,0:T(8,128)(2,1)S(1)} %broadcast_in_dim.16, s32[]{:T(128)S(6)} %select_n.13, bf16[256,512]{1,0:T(8,128)(2,1)S(1)} %get-tuple-element.9.refs_0_, ...), kind=kCustom, calls=%fused_computation.3 | custom fusion | bytes 1638404 | tf_op jit(solution)/shard_map/far/pallas_call | solution.py:175
  30.6 0.0 collective-permute-start.10
  30.6 1.5 %collective-permute-start.11 = (bf16[32,256]{1,0:T(8,128)(2,1)S(1)}, bf16[32,256]{1,0:T(8,128)(2,1)S(1)}, u32[]{:S(2)}, u32[]{:S(2)}) collective-permute-start(bf16[32,256]{1,0:T(8,128)(2,1)S(1)} %get-tuple-element.21), channel_id=1, source_target_pairs={{0,2},{1,3},{2,0},{3,1},{4,6},{5,7},{6,4},{7,5},{8,10},{9,11},{10,... | collective-permute-start | bytes 49160 | tf_op jit(solution)/shard_map/ppermute | solution.py:23
  32.0 0.4 collective-permute-start.12
  32.4 4.4 %all-to-all-start = ((f32[32,4,128]{2,1,0:T(4,128)}), f32[32,4,128]{2,1,0:T(4,128)S(1)}, u32[]{:S(2)}, u32[]{:S(2)}) async-start(f32[32,4,128]{2,1,0:T(4,128)} %bitcast.4), calls=%async_computation | async-start | bytes 131072 | tf_op jit(solution)/shard_map/all_to_all | solution.py:201
  36.8 0.0 collective-permute-done.10
  36.9 0.0 copy-start
  36.9 0.0 copy-start.1
  36.9 7.3 %all-to-all-done = f32[32,4,128]{2,1,0:T(4,128)S(1)} async-done(((f32[32,4,128]{2,1,0:T(4,128)}), f32[32,4,128]{2,1,0:T(4,128)S(1)}, u32[]{:S(2)}, u32[]{:S(2)}) %all-to-all-start) | async-done | bytes 65568 | tf_op jit(solution)/shard_map/all_to_all | solution.py:201
  44.2 0.7 %close.1 = f32[64,32]{1,0:T(8,128)} custom-call(f32[128,128]{1,0:T(8,128)S(1)} %bitcast.12, f32[64,32]{1,0:T(8,128)S(1)} %bitcast.13), custom_call_target="tpu_custom_call" | custom-call | tf_op jit(solution)/shard_map/close/pallas_call | solution.py:202
  (8 shorter events, 0.0 us)
Async XLA Ops:
  1.7 9.3 %collective-permute-start.1 = (bf16[256,512]{1,0:T(8,128)(2,1)S(1)}, bf16[256,512]{1,0:T(8,128)(2,1)S(1)}, u32[]{:S(2)}, u32[]{:S(2)}) collective-permute-start(bf16[256,512]{1,0:T(8,128)(2,1)S(1)} %get-tuple-element.9.refs_0_), channel_id=1, source_target_pairs={{0,2},{1,3},{2,0},{3,1},{4,6},{5,7},{6,4},{7,5},{8,10},{9,11},{10,... | collective-permute-start | bytes 786440 | tf_op jit(solution)/shard_map/ppermute | solution.py:23
  4.7 19.9 %collective-permute-start = (bf16[256,512]{1,0:T(8,128)(2,1)S(1)}, bf16[256,512]{1,0:T(8,128)(2,1)S(1)}, u32[]{:S(2)}, u32[]{:S(2)}) collective-permute-start(bf16[256,512]{1,0:T(8,128)(2,1)S(1)} %get-tuple-element.9.refs_0_), channel_id=1, source_target_pairs={{0,1},{1,0},{2,3},{3,2},{4,5},{5,4},{6,7},{7,6},{8,9},{9,8},{10,11... | collective-permute-start | bytes 786440 | tf_op jit(solution)/shard_map/ppermute | solution.py:23
  11.0 14.1 %collective-permute-start.2 = (bf16[256,512]{1,0:T(8,128)(2,1)S(1)}, bf16[256,512]{1,0:T(8,128)(2,1)S(1)}, u32[]{:S(2)}, u32[]{:S(2)}) collective-permute-start(bf16[256,512]{1,0:T(8,128)(2,1)S(1)} %collective-permute-done.1.refs_2_), channel_id=1, source_target_pairs={{0,1},{1,0},{2,3},{3,2},{4,5},{5,4},{6,7},{7,6},{8,9},{9,8},{10,11... | collective-permute-start | bytes 786440 | tf_op jit(solution)/shard_map/ppermute | solution.py:23
  11.0 6.9 %collective-permute-start.4 = (bf16[256,128]{1,0:T(8,128)(2,1)S(1)}, bf16[256,128]{1,0:T(8,128)(2,1)S(1)}, u32[]{:S(2)}, u32[]{:S(2)}) collective-permute-start(bf16[256,128]{1,0:T(8,128)(2,1)S(1)} %get-tuple-element.10.refs_4_), channel_id=1, source_target_pairs={{0,16},{4,20},{8,24},{12,28},{16,0},{20,4},{24,8},{28,12},{1,17},{... | collective-permute-start | bytes 196616 | tf_op jit(solution)/shard_map/ppermute | solution.py:23
  13.8 6.4 %collective-permute-start.3 = (bf16[256,128]{1,0:T(8,128)(2,1)S(1)}, bf16[256,128]{1,0:T(8,128)(2,1)S(1)}, u32[]{:S(2)}, u32[]{:S(2)}) collective-permute-start(bf16[256,128]{1,0:T(8,128)(2,1)S(1)} %get-tuple-element.10.refs_4_), channel_id=1, source_target_pairs={{0,8},{4,12},{8,0},{12,4},{16,24},{20,28},{24,16},{28,20},{1,9},{5... | collective-permute-start | bytes 196616 | tf_op jit(solution)/shard_map/ppermute | solution.py:23
  17.9 5.2 %collective-permute-start.5 = (bf16[256,128]{1,0:T(8,128)(2,1)S(1)}, bf16[256,128]{1,0:T(8,128)(2,1)S(1)}, u32[]{:S(2)}, u32[]{:S(2)}) collective-permute-start(bf16[256,128]{1,0:T(8,128)(2,1)S(1)} %collective-permute-done.4.refs_6_), channel_id=1, source_target_pairs={{0,8},{4,12},{8,0},{12,4},{16,24},{20,28},{24,16},{28,20},{1,9},{5... | collective-permute-start | bytes 196616 | tf_op jit(solution)/shard_map/ppermute | solution.py:23
  18.8 6.6 %collective-permute-start.6 = (bf16[256,128]{1,0:T(8,128)(2,1)S(1)}, bf16[256,128]{1,0:T(8,128)(2,1)S(1)}, u32[]{:S(2)}, u32[]{:S(2)}) collective-permute-start(bf16[256,128]{1,0:T(8,128)(2,1)S(1)} %get-tuple-element.10.refs_4_), channel_id=1, source_target_pairs={{0,4},{4,0},{8,12},{12,8},{16,20},{20,16},{24,28},{28,24},{1,5},{5... | collective-permute-start | bytes 196616 | tf_op jit(solution)/shard_map/ppermute | solution.py:23
  20.3 7.1 %collective-permute-start.9 = (bf16[256,128]{1,0:T(8,128)(2,1)S(1)}, bf16[256,128]{1,0:T(8,128)(2,1)S(1)}, u32[]{:S(2)}, u32[]{:S(2)}) collective-permute-start(bf16[256,128]{1,0:T(8,128)(2,1)S(1)} %get-tuple-element.10.refs_4_), channel_id=1, source_target_pairs={{0,28},{4,24},{8,20},{12,16},{16,12},{20,8},{24,4},{28,0},{1,29},{... | collective-permute-start | bytes 196616 | tf_op jit(solution)/shard_map/ppermute | solution.py:23
  23.0 5.5 %collective-permute-start.8 = (bf16[256,128]{1,0:T(8,128)(2,1)S(1)}, bf16[256,128]{1,0:T(8,128)(2,1)S(1)}, u32[]{:S(2)}, u32[]{:S(2)}) collective-permute-start(bf16[256,128]{1,0:T(8,128)(2,1)S(1)} %collective-permute-done.4.refs_6_), channel_id=1, source_target_pairs={{0,4},{4,0},{8,12},{12,8},{16,20},{20,16},{24,28},{28,24},{1,5},{5... | collective-permute-start | bytes 196616 | tf_op jit(solution)/shard_map/ppermute | solution.py:23
  24.5 4.7 %collective-permute-start.7 = (bf16[256,128]{1,0:T(8,128)(2,1)S(1)}, bf16[256,128]{1,0:T(8,128)(2,1)S(1)}, u32[]{:S(2)}, u32[]{:S(2)}) collective-permute-start(bf16[256,128]{1,0:T(8,128)(2,1)S(1)} %collective-permute-done.3.refs_5_), channel_id=1, source_target_pairs={{0,4},{4,0},{8,12},{12,8},{16,20},{20,16},{24,28},{28,24},{1,5},{5... | collective-permute-start | bytes 196616 | tf_op jit(solution)/shard_map/ppermute | solution.py:23
  30.6 6.3 %collective-permute-start.10 = (bf16[32,256]{1,0:T(8,128)(2,1)S(1)}, bf16[32,256]{1,0:T(8,128)(2,1)S(1)}, u32[]{:S(2)}, u32[]{:S(2)}) collective-permute-start(bf16[32,256]{1,0:T(8,128)(2,1)S(1)} %get-tuple-element.19), channel_id=1, source_target_pairs={{0,1},{1,0},{2,3},{3,2},{4,5},{5,4},{6,7},{7,6},{8,9},{9,8},{10,11... | collective-permute-start | bytes 49160 | tf_op jit(solution)/shard_map/ppermute | solution.py:23
  30.6 6.3 %collective-permute-start.11 = (bf16[32,256]{1,0:T(8,128)(2,1)S(1)}, bf16[32,256]{1,0:T(8,128)(2,1)S(1)}, u32[]{:S(2)}, u32[]{:S(2)}) collective-permute-start(bf16[32,256]{1,0:T(8,128)(2,1)S(1)} %get-tuple-element.21), channel_id=1, source_target_pairs={{0,2},{1,3},{2,0},{3,1},{4,6},{5,7},{6,4},{7,5},{8,10},{9,11},{10,... | collective-permute-start | bytes 49160 | tf_op jit(solution)/shard_map/ppermute | solution.py:23
  32.0 4.9 %collective-permute-start.12 = (bf16[32,256]{1,0:T(8,128)(2,1)S(1)}, bf16[32,256]{1,0:T(8,128)(2,1)S(1)}, u32[]{:S(2)}, u32[]{:S(2)}) collective-permute-start(bf16[32,256]{1,0:T(8,128)(2,1)S(1)} %get-tuple-element.23), channel_id=1, source_target_pairs={{0,3},{1,2},{2,1},{3,0},{4,7},{5,6},{6,5},{7,4},{8,11},{9,10},{10,... | collective-permute-start | bytes 49160 | tf_op jit(solution)/shard_map/ppermute | solution.py:23
  32.4 11.8 %all-to-all-start = ((f32[32,4,128]{2,1,0:T(4,128)}), f32[32,4,128]{2,1,0:T(4,128)S(1)}, u32[]{:S(2)}, u32[]{:S(2)}) async-start(f32[32,4,128]{2,1,0:T(4,128)} %bitcast.4), calls=%async_computation | async-start | bytes 131072 | tf_op jit(solution)/shard_map/all_to_all | solution.py:201
  36.9 7.4 %copy-start = (f32[4,16,32]{2,1,0:T(8,128)S(1)}, f32[4,16,32]{2,1,0:T(8,128)}, u32[]{:S(2)}) copy-start(f32[4,16,32]{2,1,0:T(8,128)} %param.7) | copy-start | bytes 24580
  36.9 8.0 %copy-start.1 = (bf16[4,32,256]{2,1,0:T(8,128)(2,1)}, bf16[4,32,256]{2,1,0:T(8,128)(2,1)S(1)}, u32[]{:S(2)}) copy-start(bf16[4,32,256]{2,1,0:T(8,128)(2,1)S(1)} %bitcast_dynamic-update-slice_fusion) | copy-start | bytes 196612

commit v2 on v1

--- a/solution.py
+++ b/solution.py
@@ -80,18 +80,10 @@
 def far_kernel(n_col, dense, *refs):
     blocks = refs[:n_col]
     near_ref, own_ref = refs[n_col : n_col + 2]
-    held, refs = refs[n_col + 2 : -4 - n_col], refs[-4 - n_col :]
-    packed_ref, sends = refs[0], refs[1 : 1 + n_col]
-    turned_ref, inner_ref, level_ref = refs[1 + n_col :]
+    held, (packed_ref, total_ref, inner_ref, level_ref) = refs[n_col + 2 : -4], refs[-4:]
     fill(level_ref, held, 1)
-    col = lax.axis_index("col")
     total = add_products(near_ref[...], blocks, level_ref, 1 - lax.axis_index("row") % 2)
-
-    tall = turned_ref.shape[0] // n_col
-    turned_ref[...] = jnp.transpose(-total).astype(jnp.bfloat16)
-    for distance in range(n_col):
-        start = pl.multiple_of((col ^ distance) * tall, tall)
-        sends[distance][...] = turned_ref[pl.ds(start, tall), :]
+    total_ref[...] = total
 
     high = total.astype(jnp.bfloat16)
     low = (total - high.astype(jnp.float32)).astype(jnp.bfloat16)
@@ -115,6 +107,16 @@
             packed_ref[pl.ds(4 * owner + a, 8, stride=16), :] = piece
 
 
+def turn_kernel(total_ref, *refs):
+    sends, turned_ref = refs[:-1], refs[-1]
+    col = lax.axis_index("col")
+    tall = sends[0].shape[0]
+    turned_ref[...] = jnp.transpose(-total_ref[...]).astype(jnp.bfloat16)
+    for distance, send_ref in enumerate(sends):
+        start = pl.multiple_of((col ^ distance) * tall, tall)
+        send_ref[...] = turned_ref[pl.ds(start, tall), :]
+
+
 def close_kernel(packed_ref, diag_ref, out_ref):
     total = packed_ref[pl.ds(0, 16), :]
     for row in range(1, 8):
@@ -172,20 +174,27 @@
         compiler_params=PARAMS,
         name="near",
     )(*blocks, *(held[d] for d in range(0, n_row, 2)))
-    packed, *sends = pl.pallas_call(
+    packed, total = pl.pallas_call(
         functools.partial(far_kernel, n_col, dense),
-        out_shape=[shape((width, width), jnp.float32)]
-        + [shape((wide, rows), jnp.bfloat16)] * n_col,
+        out_shape=[
+            shape((width, width), jnp.float32),
+            shape((rows, width), jnp.float32),
+        ],
         in_specs=[VMEM] * (n_col + 2 + n_row // 2),
-        out_specs=[VMEM] * (n_col + 1),
-        scratch_shapes=[
-            pltpu.VMEM((width, rows), jnp.bfloat16),
-            pltpu.VMEM((width, width), jnp.float32),
-            level,
-        ],
+        out_specs=[VMEM] * 2,
+        scratch_shapes=[pltpu.VMEM((width, width), jnp.float32), level],
         compiler_params=PARAMS,
         name="far",
     )(*blocks, total, own, *(held[d] for d in range(1, n_row, 2)))
+    sends = pl.pallas_call(
+        turn_kernel,
+        out_shape=[shape((wide, rows), jnp.bfloat16)] * n_col,
+        in_specs=[VMEM],
+        out_specs=[VMEM] * n_col,
+        scratch_shapes=[pltpu.VMEM((width, rows), jnp.bfloat16)],
+        compiler_params=PARAMS,
+        name="turn",
+    )(total)
 
     col = lax.axis_index("col")
     panel = jnp.zeros((n_col, wide, rows), jnp.bfloat16)

time: 45.1 us -> 45.3 us (level)
  Pallas kernels: 2.03 us -> 3.26 us
  local copies, waits for them, and re-layouts: 1.32 us -> 0.15 us
    pallas_call x0 -> x1, Pallas kernels: none -> 1.24 us  [on_device(): pl.pallas_call(functools.partial(far_kernel, n_col, dense), out_shape=[sh...]
    pallas_call x1, local copies, waits for them, and re-layouts: 1.28 us -> 0.11 us  [on_device(): pl.pallas_call(turn_kernel, out_shape=[shape((wide, rows), jnp.bfloat16)]...]
where the time goes in v2:
time: 45.3 us; the launch traced here: 45.1 us
  starting transfers between devices  20.9 us (46%)
  waiting for transfers between devices  19.9 us (44%)
  Pallas kernels  3.26 us (7%)
  between operations  0.77 us (2%)
    ppermute x13, starting transfers between devices, swap(): return lax.ppermute(block, axis, [(i, i ^ distance) for i in range(size)])  16.5 us
    ppermute x13, waiting for transfers between devices, swap(): return lax.ppermute(block, axis, [(i, i ^ distance) for i in range(size)])  12.6 us
    all_to_all x1, waiting for transfers between devices, on_device(): packed = lax.all_to_all(packed, axes, 0, 0, tiled=True)  7.3 us
    all_to_all x1, starting transfers between devices, on_device(): packed = lax.all_to_all(packed, axes, 0, 0, tiled=True)  4.41 us
    pallas_call x1, Pallas kernels, on_device(): pl.pallas_call(functools.partial(far_kernel, n_col, dense), out_shape=[sh...  1.24 us
    pallas_call x1, Pallas kernels, on_device(): pl.pallas_call(mask_kernel, out_shape=[shape((rows, width), jnp.bfloat16)...  1.02 us
  transfers between devices with their start and end apart: 14, of which 6 were waited for; matrix products, arithmetic and copies ran while one was open for 0% of the time, Pallas kernels for 1%

profile of v2, /device:TPU:0, one launch (start us, length us, event | category | flops | bytes accessed | tf_op | source)
XLA Modules:
  0.0 45.1 jit_solution(7241646408985267251)
XLA Ops:
  0.6 1.0 %mask.1 = (bf16[256,128]{1,0:T(8,128)(2,1)S(1)}, bf16[256,512]{1,0:T(8,128)(2,1)S(1)}) custom-call(s32[1,2]{1,0:T(1,128)} %pattern_ref.1, bf16[1,256,128]{2,1,0:T(8,128)(2,1)} %factor_ref.1, bf16[256,512]{1,0:T(8,128)(2,1)} %inv_ref.1), custom_call_target="tpu_custom_call" | custom-call | tf_op jit(solution)/shard_map/mask/pallas_call | solution.py:138
  1.7 3.0 %collective-permute-start.1 = (bf16[256,512]{1,0:T(8,128)(2,1)S(1)}, bf16[256,512]{1,0:T(8,128)(2,1)S(1)}, u32[]{:S(2)}, u32[]{:S(2)}) collective-permute-start(bf16[256,512]{1,0:T(8,128)(2,1)S(1)} %get-tuple-element.10.refs_0_), channel_id=1, source_target_pairs={{0,2},{1,3},{2,0},{3,1},{4,6},{5,7},{6,4},{7,5},{8,10},{9,11},{10,... | collective-permute-start | bytes 786440 | tf_op jit(solution)/shard_map/ppermute | solution.py:23
  4.7 0.0 collective-permute-start
  4.7 6.3 %collective-permute-done.1.refs_2_ = bf16[256,512]{1,0:T(8,128)(2,1)S(1)} collective-permute-done((bf16[256,512]{1,0:T(8,128)(2,1)S(1)}, bf16[256,512]{1,0:T(8,128)(2,1)S(1)}, u32[]{:S(2)}, u32[]{:S(2)}) %collective-permute-start.1) | collective-permute-done | bytes 262176 | tf_op jit(solution)/shard_map/ppermute | solution.py:23
  11.0 0.0 collective-permute-start.2
  11.0 2.8 %collective-permute-start.4 = (bf16[256,128]{1,0:T(8,128)(2,1)S(1)}, bf16[256,128]{1,0:T(8,128)(2,1)S(1)}, u32[]{:S(2)}, u32[]{:S(2)}) collective-permute-start(bf16[256,128]{1,0:T(8,128)(2,1)S(1)} %get-tuple-element.11.refs_4_.refs_5_), channel_id=1, source_target_pairs={{0,16},{4,20},{8,24},{12,28},{16,0},{20,4},{24,8},{28,12},{1,17},{... | collective-permute-start | bytes 196616 | tf_op jit(solution)/shard_map/ppermute | solution.py:23
  13.8 1.6 %collective-permute-start.3 = (bf16[256,128]{1,0:T(8,128)(2,1)S(1)}, bf16[256,128]{1,0:T(8,128)(2,1)S(1)}, u32[]{:S(2)}, u32[]{:S(2)}) collective-permute-start(bf16[256,128]{1,0:T(8,128)(2,1)S(1)} %get-tuple-element.11.refs_4_.refs_5_), channel_id=1, source_target_pairs={{0,8},{4,12},{8,0},{12,4},{16,24},{20,28},{24,16},{28,20},{1,9},{5... | collective-permute-start | bytes 196616 | tf_op jit(solution)/shard_map/ppermute | solution.py:23
  15.4 2.4 %collective-permute-done.4.refs_6_ = bf16[256,128]{1,0:T(8,128)(2,1)S(1)} collective-permute-done((bf16[256,128]{1,0:T(8,128)(2,1)S(1)}, bf16[256,128]{1,0:T(8,128)(2,1)S(1)}, u32[]{:S(2)}, u32[]{:S(2)}) %collective-permute-start.4) | collective-permute-done | bytes 65568 | tf_op jit(solution)/shard_map/ppermute | solution.py:23
  17.9 0.9 %collective-permute-start.5 = (bf16[256,128]{1,0:T(8,128)(2,1)S(1)}, bf16[256,128]{1,0:T(8,128)(2,1)S(1)}, u32[]{:S(2)}, u32[]{:S(2)}) collective-permute-start(bf16[256,128]{1,0:T(8,128)(2,1)S(1)} %collective-permute-done.4.refs_6_), channel_id=1, source_target_pairs={{0,8},{4,12},{8,0},{12,4},{16,24},{20,28},{24,16},{28,20},{1,9},{5... | collective-permute-start | bytes 196616 | tf_op jit(solution)/shard_map/ppermute | solution.py:23
  18.8 1.5 %collective-permute-start.6 = (bf16[256,128]{1,0:T(8,128)(2,1)S(1)}, bf16[256,128]{1,0:T(8,128)(2,1)S(1)}, u32[]{:S(2)}, u32[]{:S(2)}) collective-permute-start(bf16[256,128]{1,0:T(8,128)(2,1)S(1)} %get-tuple-element.11.refs_4_.refs_5_), channel_id=1, source_target_pairs={{0,4},{4,0},{8,12},{12,8},{16,20},{20,16},{24,28},{28,24},{1,5},{5... | collective-permute-start | bytes 196616 | tf_op jit(solution)/shard_map/ppermute | solution.py:23
  20.3 0.0 collective-permute-done.3.refs_5_
  20.3 2.7 %collective-permute-start.9 = (bf16[256,128]{1,0:T(8,128)(2,1)S(1)}, bf16[256,128]{1,0:T(8,128)(2,1)S(1)}, u32[]{:S(2)}, u32[]{:S(2)}) collective-permute-start(bf16[256,128]{1,0:T(8,128)(2,1)S(1)} %get-tuple-element.11.refs_4_.refs_5_), channel_id=1, source_target_pairs={{0,28},{4,24},{8,20},{12,16},{16,12},{20,8},{24,4},{28,0},{1,29},{... | collective-permute-start | bytes 196616 | tf_op jit(solution)/shard_map/ppermute | solution.py:23
  23.0 0.0 collective-permute-done.5.refs_7_
  23.0 1.5 %collective-permute-start.8 = (bf16[256,128]{1,0:T(8,128)(2,1)S(1)}, bf16[256,128]{1,0:T(8,128)(2,1)S(1)}, u32[]{:S(2)}, u32[]{:S(2)}) collective-permute-start(bf16[256,128]{1,0:T(8,128)(2,1)S(1)} %collective-permute-done.4.refs_6_), channel_id=1, source_target_pairs={{0,4},{4,0},{8,12},{12,8},{16,20},{20,16},{24,28},{28,24},{1,5},{5... | collective-permute-start | bytes 196616 | tf_op jit(solution)/shard_map/ppermute | solution.py:23
  24.5 0.5 %collective-permute-start.7 = (bf16[256,128]{1,0:T(8,128)(2,1)S(1)}, bf16[256,128]{1,0:T(8,128)(2,1)S(1)}, u32[]{:S(2)}, u32[]{:S(2)}) collective-permute-start(bf16[256,128]{1,0:T(8,128)(2,1)S(1)} %collective-permute-done.3.refs_5_), channel_id=1, source_target_pairs={{0,4},{4,0},{8,12},{12,8},{16,20},{20,16},{24,28},{28,24},{1,5},{5... | collective-permute-start | bytes 196616 | tf_op jit(solution)/shard_map/ppermute | solution.py:23
  25.0 0.3 near.1.refs_4_
  25.4 0.0 collective-permute-done.6.refs_6_
  25.4 2.0 %collective-permute-done.9.refs_9_ = bf16[256,128]{1,0:T(8,128)(2,1)S(1)} collective-permute-done((bf16[256,128]{1,0:T(8,128)(2,1)S(1)}, bf16[256,128]{1,0:T(8,128)(2,1)S(1)}, u32[]{:S(2)}, u32[]{:S(2)}) %collective-permute-start.9) | collective-permute-done | bytes 65568 | tf_op jit(solution)/shard_map/ppermute | solution.py:23
  27.3 1.2 %collective-permute-done.8.refs_8_ = bf16[256,128]{1,0:T(8,128)(2,1)S(1)} collective-permute-done((bf16[256,128]{1,0:T(8,128)(2,1)S(1)}, bf16[256,128]{1,0:T(8,128)(2,1)S(1)}, u32[]{:S(2)}, u32[]{:S(2)}) %collective-permute-start.8) | collective-permute-done | bytes 65568 | tf_op jit(solution)/shard_map/ppermute | solution.py:23
  28.6 0.7 %collective-permute-done.7.refs_7_ = bf16[256,128]{1,0:T(8,128)(2,1)S(1)} collective-permute-done((bf16[256,128]{1,0:T(8,128)(2,1)S(1)}, bf16[256,128]{1,0:T(8,128)(2,1)S(1)}, u32[]{:S(2)}, u32[]{:S(2)}) %collective-permute-start.7) | collective-permute-done | bytes 65568 | tf_op jit(solution)/shard_map/ppermute | solution.py:23
  29.3 1.2 %far.1 = (f32[128,128]{1,0:T(8,128)}, f32[256,128]{1,0:T(8,128)S(1)}) custom-call(bf16[256,512]{1,0:T(8,128)(2,1)S(1)} %get-tuple-element.10.refs_0_, bf16[256,512]{1,0:T(8,128)(2,1)S(1)} %collective-permute-done.refs_1_, bf16[256,512]{1,0:T(8,128)(2,1)S(1)} %collective-permute-done.1.refs_2_, bf16[256,512]{1,0:T(8,128)(2,1)S(1)} %collective-permute-done.2.refs_3_, ...), custom_call_target="tpu_custom_call" | custom-call | tf_op jit(solution)/shard_map/far/pallas_call | solution.py:177
  30.5 0.1 turn.1
  30.6 0.1 collective-permute-start.10
  30.7 1.6 %collective-permute-start.11 = (bf16[32,256]{1,0:T(8,128)(2,1)S(1)}, bf16[32,256]{1,0:T(8,128)(2,1)S(1)}, u32[]{:S(2)}, u32[]{:S(2)}) collective-permute-start(bf16[32,256]{1,0:T(8,128)(2,1)S(1)} %get-tuple-element.23), channel_id=1, source_target_pairs={{0,2},{1,3},{2,0},{3,1},{4,6},{5,7},{6,4},{7,5},{8,10},{9,11},{10,... | collective-permute-start | bytes 49160 | tf_op jit(solution)/shard_map/ppermute | solution.py:23
  32.3 0.3 collective-permute-start.12
  32.6 4.4 %all-to-all-start = ((f32[32,4,128]{2,1,0:T(4,128)}), f32[32,4,128]{2,1,0:T(4,128)S(1)}, u32[]{:S(2)}, u32[]{:S(2)}) async-start(f32[32,4,128]{2,1,0:T(4,128)} %bitcast.4), calls=%async_computation | async-start | bytes 131072 | tf_op jit(solution)/shard_map/all_to_all | solution.py:210
  37.0 0.0 copy-start
  37.0 0.0 collective-permute-done.11
  37.0 0.0 collective-permute-done.12
  37.1 0.0 copy-start.1
  37.1 7.3 %all-to-all-done = f32[32,4,128]{2,1,0:T(4,128)S(1)} async-done(((f32[32,4,128]{2,1,0:T(4,128)}), f32[32,4,128]{2,1,0:T(4,128)S(1)}, u32[]{:S(2)}, u32[]{:S(2)}) %all-to-all-start) | async-done | bytes 65568 | tf_op jit(solution)/shard_map/all_to_all | solution.py:210
  44.4 0.7 %close.1 = f32[64,32]{1,0:T(8,128)} custom-call(f32[128,128]{1,0:T(8,128)S(1)} %bitcast.12, f32[64,32]{1,0:T(8,128)S(1)} %bitcast.13), custom_call_target="tpu_custom_call" | custom-call | tf_op jit(solution)/shard_map/close/pallas_call | solution.py:211
  (9 shorter events, 0.0 us)
Async XLA Ops:
  1.7 9.3 %collective-permute-start.1 = (bf16[256,512]{1,0:T(8,128)(2,1)S(1)}, bf16[256,512]{1,0:T(8,128)(2,1)S(1)}, u32[]{:S(2)}, u32[]{:S(2)}) collective-permute-start(bf16[256,512]{1,0:T(8,128)(2,1)S(1)} %get-tuple-element.10.refs_0_), channel_id=1, source_target_pairs={{0,2},{1,3},{2,0},{3,1},{4,6},{5,7},{6,4},{7,5},{8,10},{9,11},{10,... | collective-permute-start | bytes 786440 | tf_op jit(solution)/shard_map/ppermute | solution.py:23
  4.7 19.9 %collective-permute-start = (bf16[256,512]{1,0:T(8,128)(2,1)S(1)}, bf16[256,512]{1,0:T(8,128)(2,1)S(1)}, u32[]{:S(2)}, u32[]{:S(2)}) collective-permute-start(bf16[256,512]{1,0:T(8,128)(2,1)S(1)} %get-tuple-element.10.refs_0_), channel_id=1, source_target_pairs={{0,1},{1,0},{2,3},{3,2},{4,5},{5,4},{6,7},{7,6},{8,9},{9,8},{10,11... | collective-permute-start | bytes 786440 | tf_op jit(solution)/shard_map/ppermute | solution.py:23
  11.0 14.1 %collective-permute-start.2 = (bf16[256,512]{1,0:T(8,128)(2,1)S(1)}, bf16[256,512]{1,0:T(8,128)(2,1)S(1)}, u32[]{:S(2)}, u32[]{:S(2)}) collective-permute-start(bf16[256,512]{1,0:T(8,128)(2,1)S(1)} %collective-permute-done.1.refs_2_), channel_id=1, source_target_pairs={{0,1},{1,0},{2,3},{3,2},{4,5},{5,4},{6,7},{7,6},{8,9},{9,8},{10,11... | collective-permute-start | bytes 786440 | tf_op jit(solution)/shard_map/ppermute | solution.py:23
  11.0 6.9 %collective-permute-start.4 = (bf16[256,128]{1,0:T(8,128)(2,1)S(1)}, bf16[256,128]{1,0:T(8,128)(2,1)S(1)}, u32[]{:S(2)}, u32[]{:S(2)}) collective-permute-start(bf16[256,128]{1,0:T(8,128)(2,1)S(1)} %get-tuple-element.11.refs_4_.refs_5_), channel_id=1, source_target_pairs={{0,16},{4,20},{8,24},{12,28},{16,0},{20,4},{24,8},{28,12},{1,17},{... | collective-permute-start | bytes 196616 | tf_op jit(solution)/shard_map/ppermute | solution.py:23
  13.8 6.4 %collective-permute-start.3 = (bf16[256,128]{1,0:T(8,128)(2,1)S(1)}, bf16[256,128]{1,0:T(8,128)(2,1)S(1)}, u32[]{:S(2)}, u32[]{:S(2)}) collective-permute-start(bf16[256,128]{1,0:T(8,128)(2,1)S(1)} %get-tuple-element.11.refs_4_.refs_5_), channel_id=1, source_target_pairs={{0,8},{4,12},{8,0},{12,4},{16,24},{20,28},{24,16},{28,20},{1,9},{5... | collective-permute-start | bytes 196616 | tf_op jit(solution)/shard_map/ppermute | solution.py:23
  17.9 5.2 %collective-permute-start.5 = (bf16[256,128]{1,0:T(8,128)(2,1)S(1)}, bf16[256,128]{1,0:T(8,128)(2,1)S(1)}, u32[]{:S(2)}, u32[]{:S(2)}) collective-permute-start(bf16[256,128]{1,0:T(8,128)(2,1)S(1)} %collective-permute-done.4.refs_6_), channel_id=1, source_target_pairs={{0,8},{4,12},{8,0},{12,4},{16,24},{20,28},{24,16},{28,20},{1,9},{5... | collective-permute-start | bytes 196616 | tf_op jit(solution)/shard_map/ppermute | solution.py:23
  18.8 6.6 %collective-permute-start.6 = (bf16[256,128]{1,0:T(8,128)(2,1)S(1)}, bf16[256,128]{1,0:T(8,128)(2,1)S(1)}, u32[]{:S(2)}, u32[]{:S(2)}) collective-permute-start(bf16[256,128]{1,0:T(8,128)(2,1)S(1)} %get-tuple-element.11.refs_4_.refs_5_), channel_id=1, source_target_pairs={{0,4},{4,0},{8,12},{12,8},{16,20},{20,16},{24,28},{28,24},{1,5},{5... | collective-permute-start | bytes 196616 | tf_op jit(solution)/shard_map/ppermute | solution.py:23
  20.3 7.1 %collective-permute-start.9 = (bf16[256,128]{1,0:T(8,128)(2,1)S(1)}, bf16[256,128]{1,0:T(8,128)(2,1)S(1)}, u32[]{:S(2)}, u32[]{:S(2)}) collective-permute-start(bf16[256,128]{1,0:T(8,128)(2,1)S(1)} %get-tuple-element.11.refs_4_.refs_5_), channel_id=1, source_target_pairs={{0,28},{4,24},{8,20},{12,16},{16,12},{20,8},{24,4},{28,0},{1,29},{... | collective-permute-start | bytes 196616 | tf_op jit(solution)/shard_map/ppermute | solution.py:23
  23.0 5.5 %collective-permute-start.8 = (bf16[256,128]{1,0:T(8,128)(2,1)S(1)}, bf16[256,128]{1,0:T(8,128)(2,1)S(1)}, u32[]{:S(2)}, u32[]{:S(2)}) collective-permute-start(bf16[256,128]{1,0:T(8,128)(2,1)S(1)} %collective-permute-done.4.refs_6_), channel_id=1, source_target_pairs={{0,4},{4,0},{8,12},{12,8},{16,20},{20,16},{24,28},{28,24},{1,5},{5... | collective-permute-start | bytes 196616 | tf_op jit(solution)/shard_map/ppermute | solution.py:23
  24.5 4.7 %collective-permute-start.7 = (bf16[256,128]{1,0:T(8,128)(2,1)S(1)}, bf16[256,128]{1,0:T(8,128)(2,1)S(1)}, u32[]{:S(2)}, u32[]{:S(2)}) collective-permute-start(bf16[256,128]{1,0:T(8,128)(2,1)S(1)} %collective-permute-done.3.refs_5_), channel_id=1, source_target_pairs={{0,4},{4,0},{8,12},{12,8},{16,20},{20,16},{24,28},{28,24},{1,5},{5... | collective-permute-start | bytes 196616 | tf_op jit(solution)/shard_map/ppermute | solution.py:23
  30.6 6.3 %collective-permute-start.10 = (bf16[32,256]{1,0:T(8,128)(2,1)S(1)}, bf16[32,256]{1,0:T(8,128)(2,1)S(1)}, u32[]{:S(2)}, u32[]{:S(2)}) collective-permute-start(bf16[32,256]{1,0:T(8,128)(2,1)S(1)} %get-tuple-element.21), channel_id=1, source_target_pairs={{0,1},{1,0},{2,3},{3,2},{4,5},{5,4},{6,7},{7,6},{8,9},{9,8},{10,11... | collective-permute-start | bytes 49160 | tf_op jit(solution)/shard_map/ppermute | solution.py:23
  30.7 6.3 %collective-permute-start.11 = (bf16[32,256]{1,0:T(8,128)(2,1)S(1)}, bf16[32,256]{1,0:T(8,128)(2,1)S(1)}, u32[]{:S(2)}, u32[]{:S(2)}) collective-permute-start(bf16[32,256]{1,0:T(8,128)(2,1)S(1)} %get-tuple-element.23), channel_id=1, source_target_pairs={{0,2},{1,3},{2,0},{3,1},{4,6},{5,7},{6,4},{7,5},{8,10},{9,11},{10,... | collective-permute-start | bytes 49160 | tf_op jit(solution)/shard_map/ppermute | solution.py:23
  32.3 4.8 %collective-permute-start.12 = (bf16[32,256]{1,0:T(8,128)(2,1)S(1)}, bf16[32,256]{1,0:T(8,128)(2,1)S(1)}, u32[]{:S(2)}, u32[]{:S(2)}) collective-permute-start(bf16[32,256]{1,0:T(8,128)(2,1)S(1)} %get-tuple-element.25), channel_id=1, source_target_pairs={{0,3},{1,2},{2,1},{3,0},{4,7},{5,6},{6,5},{7,4},{8,11},{9,10},{10,... | collective-permute-start | bytes 49160 | tf_op jit(solution)/shard_map/ppermute | solution.py:23
  32.6 11.8 %all-to-all-start = ((f32[32,4,128]{2,1,0:T(4,128)}), f32[32,4,128]{2,1,0:T(4,128)S(1)}, u32[]{:S(2)}, u32[]{:S(2)}) async-start(f32[32,4,128]{2,1,0:T(4,128)} %bitcast.4), calls=%async_computation | async-start | bytes 131072 | tf_op jit(solution)/shard_map/all_to_all | solution.py:210
  37.0 7.4 %copy-start = (f32[4,16,32]{2,1,0:T(8,128)S(1)}, f32[4,16,32]{2,1,0:T(8,128)}, u32[]{:S(2)}) copy-start(f32[4,16,32]{2,1,0:T(8,128)} %param.7) | copy-start | bytes 24580
  37.1 8.0 %copy-start.1 = (bf16[4,32,256]{2,1,0:T(8,128)(2,1)}, bf16[4,32,256]{2,1,0:T(8,128)(2,1)S(1)}, u32[]{:S(2)}) copy-start(bf16[4,32,256]{2,1,0:T(8,128)(2,1)S(1)} %bitcast_dynamic-update-slice_fusion) | copy-start | bytes 196612
